TPU v7x, 32 devices: a whole 2x2x4 slice. The times are simulated.
32 devices in a mesh: fsdp: 32 (over z, y, x, core).
Axes of the slice: x: 2, y: 2, z: 4, core: 2. Of those that a mesh axis runs over, the one named last changes fastest.
Arguments:
- block_input: bfloat16 [32, 196, 512], P('fsdp'), may hold values from -6 to 6
- out_cotangent: bfloat16 [32, 196, 512], P('fsdp'), may hold values from -6 to 6
- norm1_gain: bfloat16 [512], P('fsdp'), may hold values from 0.099609375 to 1.8984375
- norm1_bias: bfloat16 [512], P('fsdp'), may hold values from -3 to 3
- qkv_weight: bfloat16 [512, 1536], P('fsdp'), may hold values from -0.25 to 0.25
- qv_bias: bfloat16 [1024], P('fsdp'), may hold values from -3 to 3
- proj_weight: bfloat16 [512, 512], P('fsdp'), may hold values from -1 to 1
- proj_bias: bfloat16 [512], P('fsdp'), may hold values from -3 to 3
- norm2_gain: bfloat16 [512], P('fsdp'), may hold values from 0.099609375 to 1.8984375
- norm2_bias: bfloat16 [512], P('fsdp'), may hold values from -3 to 3
- fc1_weight: bfloat16 [512, 2048], P('fsdp'), may hold values from -0.25 to 0.25
- fc1_bias: bfloat16 [2048], P('fsdp'), may hold values from -3 to 3
- fc2_weight: bfloat16 [2048, 512], P(None, 'fsdp'), may hold values from -0.125 to 0.125
- fc2_bias: bfloat16 [512], P('fsdp'), may hold values from -3 to 3
- bias_table: bfloat16 [169, 16], replicated, may hold values from -4 to 296
- window_mask: int32 [4, 49, 49], replicated, may hold values from 0 to 1, as said below
- rel_index: int32 [49, 49], replicated, may hold values from 0 to 168
- partition: int32 [196], replicated, may hold values from 0 to 195, each once
Outputs:
- block_output: bfloat16 [32, 196, 512], P('fsdp')
- input_grad: float32 [32, 196, 512], P('fsdp')
- norm1_gain_grad: float32 [512], P('fsdp')
- norm1_bias_grad: float32 [512], P('fsdp')
- qkv_weight_grad: float32 [512, 1536], P('fsdp')
- qv_bias_grad: float32 [1024], P('fsdp')
- proj_weight_grad: float32 [512, 512], P('fsdp')
- proj_bias_grad: float32 [512], P('fsdp')
- norm2_gain_grad: float32 [512], P('fsdp')
- norm2_bias_grad: float32 [512], P('fsdp')
- fc1_weight_grad: float32 [512, 2048], P('fsdp')
- fc1_bias_grad: float32 [2048], P('fsdp')
- fc2_weight_grad: float32 [2048, 512], P(None, 'fsdp')
- fc2_bias_grad: float32 [512], P('fsdp')
- bias_table_grad: float32 [169, 16], replicated
Inputs may be any that keep to these rules, and one draw needn't show every extreme that they name: window_mask[w, i, j] is 1 exactly where positions i and j of window w carry the same region label; it is symmetric and 1 on the diagonal. `partition`: a permutation of 0 to 195.
All inputs are finite; a program needn't handle non-finite values.
Results may differ from a plain program's by a relative error of at most 0.011.
Values may be sent and summed in bfloat16 or wider, within the bound.
A program may use at most 128 MiB of HBM per device.

v0:
```python
import jax
import jax.numpy as jnp
from jax import lax
from jax.sharding import PartitionSpec as P

HEADS = 16
WINDOW = 49
WIN_IMG = 4
MICRO = 1
EPSILON = 1e-05
NEG_FILL = -1e30
ROOT_HALF = 0.7071067811865476
DENSITY = 0.3989422804014327


def normalize(values, gain_vec, shift_vec):
    center = values - jnp.mean(values, axis=-1, keepdims=True)
    inv_std = lax.rsqrt(jnp.mean(center * center, axis=-1, keepdims=True) + EPSILON)
    unit_rows = center * inv_std
    return (unit_rows * gain_vec + shift_vec, unit_rows, inv_std)


def norm_backward(grad_out, unit_rows, inv_std, gain_vec):
    scaled = grad_out * gain_vec
    grad_in = inv_std * (
        scaled
        - jnp.mean(scaled, axis=-1, keepdims=True)
        - unit_rows * jnp.mean(scaled * unit_rows, axis=-1, keepdims=True)
    )
    return (grad_in, jnp.sum(grad_out * unit_rows, axis=0), jnp.sum(grad_out, axis=0))


def gelu_parts(pre_act):
    normal_cdf = 0.5 * (1.0 + jax.scipy.special.erf(pre_act * ROOT_HALF))
    normal_pdf = jnp.exp(-0.5 * pre_act * pre_act) * DENSITY
    return (pre_act * normal_cdf, normal_cdf + pre_act * normal_pdf)


def to_windows(token_rows, partition):
    picked = jnp.take(token_rows, partition, axis=1)
    return picked.reshape(token_rows.shape[0], WIN_IMG, WINDOW, token_rows.shape[-1])


def from_windows(window_rows, inverse):
    flat_rows = window_rows.reshape(window_rows.shape[0], inverse.shape[0], window_rows.shape[-1])
    return jnp.take(flat_rows, inverse, axis=1)


def window_scores(queries, key_rows, lookups, score_scale):
    table_bias, allowed, partition, inverse = lookups
    raw = (
        jnp.einsum("bwihe,bwjhe->bwhij", queries, key_rows, preferred_element_type=jnp.float32)
        * score_scale
        + table_bias
    )
    return jnp.where(allowed, raw, NEG_FILL)


def fetch_pass_fwd(shards):
    return (
        lax.all_gather(shards[0], "fsdp", axis=0, tiled=True),
        lax.all_gather(shards[1], "fsdp", axis=0, tiled=True),
        lax.all_gather(shards[2], "fsdp", axis=0, tiled=True),
        lax.all_gather(shards[3], "fsdp", axis=0, tiled=True),
        lax.all_gather(shards[4], "fsdp", axis=0, tiled=True),
        lax.all_gather(shards[5], "fsdp", axis=0, tiled=True),
        lax.all_gather(shards[6], "fsdp", axis=0, tiled=True),
        lax.all_gather(shards[7], "fsdp", axis=0, tiled=True),
        lax.all_gather(shards[8], "fsdp", axis=0, tiled=True),
        lax.all_gather(shards[9], "fsdp", axis=0, tiled=True),
        lax.all_gather(shards[10], "fsdp", axis=1, tiled=True),
        lax.all_gather(shards[11], "fsdp", axis=0, tiled=True),
    )


def fetch_pass_bwd(shards):
    return (
        lax.all_gather(shards[0], "fsdp", axis=0, tiled=True),
        lax.all_gather(shards[1], "fsdp", axis=0, tiled=True),
        lax.all_gather(shards[2], "fsdp", axis=0, tiled=True),
        lax.all_gather(shards[3], "fsdp", axis=0, tiled=True),
        lax.all_gather(shards[4], "fsdp", axis=0, tiled=True),
        lax.all_gather(shards[5], "fsdp", axis=0, tiled=True),
        lax.all_gather(shards[6], "fsdp", axis=0, tiled=True),
        lax.all_gather(shards[7], "fsdp", axis=0, tiled=True),
        lax.all_gather(shards[8], "fsdp", axis=0, tiled=True),
        lax.all_gather(shards[9], "fsdp", axis=0, tiled=True),
        lax.all_gather(shards[10], "fsdp", axis=1, tiled=True),
        lax.all_gather(shards[11], "fsdp", axis=0, tiled=True),
    )


def scatter_whole(grads):
    return (
        lax.psum_scatter(grads[0], "fsdp", scatter_dimension=0, tiled=True),
        lax.psum_scatter(grads[1], "fsdp", scatter_dimension=0, tiled=True),
        lax.psum_scatter(grads[2], "fsdp", scatter_dimension=0, tiled=True),
        lax.psum_scatter(grads[3], "fsdp", scatter_dimension=0, tiled=True),
        lax.psum_scatter(grads[4], "fsdp", scatter_dimension=0, tiled=True),
        lax.psum_scatter(grads[5], "fsdp", scatter_dimension=0, tiled=True),
        lax.psum_scatter(grads[6], "fsdp", scatter_dimension=0, tiled=True),
        lax.psum_scatter(grads[7], "fsdp", scatter_dimension=0, tiled=True),
        lax.psum_scatter(grads[8], "fsdp", scatter_dimension=0, tiled=True),
        lax.psum_scatter(grads[9], "fsdp", scatter_dimension=0, tiled=True),
        lax.psum_scatter(grads[10], "fsdp", scatter_dimension=1, tiled=True),
        lax.psum_scatter(grads[11], "fsdp", scatter_dimension=0, tiled=True),
    )


def forward_pass(images, params, lookups):
    (
        gain_one,
        shift_one,
        qkv_weight,
        qv_bias,
        proj_weight,
        proj_bias,
        gain_two,
        shift_two,
        fc1_weight,
        fc1_bias,
        fc2_weight,
        fc2_bias,
    ) = params
    table_bias, allowed, partition, inverse = lookups
    image_count, tok_count, model_width = images.shape
    row_count = image_count * tok_count
    head_width = model_width // HEADS
    score_scale = head_width ** (-0.5)
    inputs_f = images.astype(jnp.float32).reshape(row_count, model_width)
    normed_one, unit_one, inv_one = normalize(
        inputs_f, gain_one.astype(jnp.float32), shift_one.astype(jnp.float32)
    )
    normed_one = normed_one.astype(jnp.bfloat16)
    qkv_shift = jnp.concatenate(
        [
            qv_bias[:model_width].astype(jnp.float32),
            jnp.zeros((model_width,), jnp.float32),
            qv_bias[model_width:].astype(jnp.float32),
        ]
    )
    qkv_rows = (
        jnp.dot(normed_one, qkv_weight, preferred_element_type=jnp.float32) + qkv_shift
    ).astype(jnp.bfloat16)
    qkv_win = to_windows(
        qkv_rows.reshape(image_count, tok_count, 3 * model_width), partition
    ).reshape(image_count, WIN_IMG, WINDOW, 3, HEADS, head_width)
    scores = window_scores(qkv_win[:, :, :, 0], qkv_win[:, :, :, 1], lookups, score_scale)
    row_top = jnp.max(scores, axis=-1, keepdims=True)
    log_total = row_top + jnp.log(jnp.sum(jnp.exp(scores - row_top), axis=-1, keepdims=True))
    soft_probs = jnp.exp(scores - log_total).astype(jnp.bfloat16)
    mixed = jnp.einsum(
        "bwhij,bwjhe->bwihe", soft_probs, qkv_win[:, :, :, 2], preferred_element_type=jnp.float32
    )
    attended = (
        from_windows(mixed.reshape(image_count, WIN_IMG, WINDOW, model_width), inverse)
        .astype(jnp.bfloat16)
        .reshape(row_count, model_width)
    )
    resid = (
        inputs_f
        + jnp.dot(attended, proj_weight, preferred_element_type=jnp.float32)
        + proj_bias.astype(jnp.float32)
    )
    normed_two, unit_two, inv_two = normalize(
        resid, gain_two.astype(jnp.float32), shift_two.astype(jnp.float32)
    )
    normed_two = normed_two.astype(jnp.bfloat16)
    pre_act = jnp.dot(normed_two, fc1_weight, preferred_element_type=jnp.float32) + fc1_bias.astype(
        jnp.float32
    )
    activ, gelu_slope = gelu_parts(pre_act)
    activ = activ.astype(jnp.bfloat16)
    output = (
        resid
        + jnp.dot(activ, fc2_weight, preferred_element_type=jnp.float32)
        + fc2_bias.astype(jnp.float32)
    ).astype(jnp.bfloat16)
    saved = (
        unit_one,
        inv_one,
        normed_one,
        qkv_win,
        log_total,
        attended,
        unit_two,
        inv_two,
        normed_two,
        gelu_slope,
        activ,
    )
    return (output.reshape(image_count, tok_count, model_width), saved)


def backward_pass(cotangent, saved, params, lookups):
    (
        gain_one,
        shift_one,
        qkv_weight,
        qv_bias,
        proj_weight,
        proj_bias,
        gain_two,
        shift_two,
        fc1_weight,
        fc1_bias,
        fc2_weight,
        fc2_bias,
    ) = params
    (
        unit_one,
        inv_one,
        normed_one,
        qkv_win,
        log_total,
        attended,
        unit_two,
        inv_two,
        normed_two,
        gelu_slope,
        activ,
    ) = saved
    table_bias, allowed, partition, inverse = lookups
    image_count, tok_count, model_width = cotangent.shape
    row_count = image_count * tok_count
    head_width = model_width // HEADS
    score_scale = head_width ** (-0.5)
    cot_rows = cotangent.reshape(row_count, model_width)
    cot_f = cot_rows.astype(jnp.float32)
    fc2_grad = jnp.dot(activ.T, cot_rows, preferred_element_type=jnp.float32)
    fc2_bias_grad = jnp.sum(cot_f, axis=0)
    grad_pre = jnp.dot(cot_rows, fc2_weight.T, preferred_element_type=jnp.float32) * gelu_slope
    grad_pre_b = grad_pre.astype(jnp.bfloat16)
    fc1_grad = jnp.dot(normed_two.T, grad_pre_b, preferred_element_type=jnp.float32)
    fc1_bias_grad = jnp.sum(grad_pre, axis=0)
    grad_normed = jnp.dot(grad_pre_b, fc1_weight.T, preferred_element_type=jnp.float32)
    grad_mid, gain_two_grad, shift_two_grad = norm_backward(
        grad_normed, unit_two, inv_two, gain_two.astype(jnp.float32)
    )
    grad_resid = cot_f + grad_mid
    grad_resid_b = grad_resid.astype(jnp.bfloat16)
    proj_grad = jnp.dot(attended.T, grad_resid_b, preferred_element_type=jnp.float32)
    proj_bias_grad = jnp.sum(grad_resid, axis=0)
    grad_att = jnp.dot(grad_resid_b, proj_weight.T, preferred_element_type=jnp.float32).astype(
        jnp.bfloat16
    )
    grad_mixed = to_windows(
        grad_att.reshape(image_count, tok_count, model_width), partition
    ).reshape(image_count, WIN_IMG, WINDOW, HEADS, head_width)
    queries = qkv_win[:, :, :, 0]
    key_rows = qkv_win[:, :, :, 1]
    value_rows = qkv_win[:, :, :, 2]
    scores = window_scores(queries, key_rows, lookups, score_scale)
    soft_full = jnp.exp(scores - log_total)
    soft_probs = soft_full.astype(jnp.bfloat16)
    value_grad = jnp.einsum(
        "bwhij,bwihe->bwjhe", soft_probs, grad_mixed, preferred_element_type=jnp.float32
    )
    prob_grad = jnp.einsum(
        "bwihe,bwjhe->bwhij", grad_mixed, value_rows, preferred_element_type=jnp.float32
    )
    score_grad = soft_full * (prob_grad - jnp.sum(soft_full * prob_grad, axis=-1, keepdims=True))
    pair_grad = jnp.sum(score_grad, axis=(0, 1))
    score_grad_b = score_grad.astype(jnp.bfloat16)
    query_grad = (
        jnp.einsum("bwhij,bwjhe->bwihe", score_grad_b, key_rows, preferred_element_type=jnp.float32)
        * score_scale
    )
    key_grad = (
        jnp.einsum("bwhij,bwihe->bwjhe", score_grad_b, queries, preferred_element_type=jnp.float32)
        * score_scale
    )
    stacked = jnp.stack([query_grad, key_grad, value_grad], axis=3).reshape(
        image_count, WIN_IMG, WINDOW, 3 * model_width
    )
    qkv_grad = from_windows(stacked, inverse).reshape(row_count, 3 * model_width)
    qkv_grad_b = qkv_grad.astype(jnp.bfloat16)
    qkv_grad_w = jnp.dot(normed_one.T, qkv_grad_b, preferred_element_type=jnp.float32)
    column_sums = jnp.sum(qkv_grad, axis=0)
    qv_grad = jnp.concatenate([column_sums[:model_width], column_sums[2 * model_width :]])
    grad_first = jnp.dot(qkv_grad_b, qkv_weight.T, preferred_element_type=jnp.float32)
    grad_low, gain_one_grad, shift_one_grad = norm_backward(
        grad_first, unit_one, inv_one, gain_one.astype(jnp.float32)
    )
    input_grad = (grad_resid + grad_low).reshape(image_count, tok_count, model_width)
    grads = (
        gain_one_grad,
        shift_one_grad,
        qkv_grad_w,
        qv_grad,
        proj_grad,
        proj_bias_grad,
        gain_two_grad,
        shift_two_grad,
        fc1_grad,
        fc1_bias_grad,
        fc2_grad,
        fc2_bias_grad,
    )
    return (input_grad, grads, pair_grad)


def per_device(
    block_input,
    out_cotangent,
    norm1_gain,
    norm1_bias,
    qkv_weight,
    qv_bias,
    proj_weight,
    proj_bias,
    norm2_gain,
    norm2_bias,
    fc1_weight,
    fc1_bias,
    fc2_weight,
    fc2_bias,
    bias_table,
    window_mask,
    rel_index,
    partition,
):
    shards = (
        norm1_gain,
        norm1_bias,
        qkv_weight,
        qv_bias,
        proj_weight,
        proj_bias,
        norm2_gain,
        norm2_bias,
        fc1_weight,
        fc1_bias,
        fc2_weight,
        fc2_bias,
    )
    pair_count = WINDOW * WINDOW
    table_rows = bias_table.shape[0]
    one_hot = (
        rel_index.reshape(pair_count, 1) == jnp.arange(table_rows, dtype=jnp.int32)[None, :]
    ).astype(jnp.float32)
    table_bias = jnp.transpose(
        jnp.dot(one_hot, bias_table.astype(jnp.float32), precision=lax.Precision.HIGHEST).reshape(
            WINDOW, WINDOW, HEADS
        ),
        (2, 0, 1),
    )
    allowed = (window_mask == 1)[None, :, None, :, :]
    tok_count = partition.shape[0]
    inverse = (
        jnp.zeros((tok_count,), jnp.int32).at[partition].set(jnp.arange(tok_count, dtype=jnp.int32))
    )
    lookups = (table_bias, allowed, partition, inverse)
    held_params = fetch_pass_fwd(shards)
    micro_index = 0
    output, saved = forward_pass(block_input, held_params, lookups)
    kept = [saved]
    held_params = fetch_pass_bwd(shards)
    input_grads = [None] * MICRO
    pair_total = jnp.zeros((HEADS, WINDOW, WINDOW), jnp.float32)
    grad_totals = None
    for micro_index in reversed(range(MICRO)):
        input_grad, grads, pair_grad = backward_pass(
            out_cotangent, kept[micro_index], held_params, lookups
        )
        input_grads[micro_index] = input_grad
        pair_total = pair_grad
        grad_totals = grads
    grad_totals = scatter_whole(grad_totals)
    table_local = jnp.dot(
        one_hot.T,
        jnp.transpose(pair_total, (1, 2, 0)).reshape(pair_count, HEADS),
        precision=lax.Precision.HIGHEST,
    )
    table_grad = lax.psum(table_local, "fsdp")
    input_grad_all = input_grads[0]
    return (
        output,
        input_grad_all,
        grad_totals[0],
        grad_totals[1],
        grad_totals[2],
        grad_totals[3],
        grad_totals[4],
        grad_totals[5],
        grad_totals[6],
        grad_totals[7],
        grad_totals[8],
        grad_totals[9],
        grad_totals[10],
        grad_totals[11],
        table_grad,
    )


def solution(mesh):
    placed = (
        P("fsdp", None, None),
        P("fsdp", None, None),
        P("fsdp"),
        P("fsdp"),
        P("fsdp", None),
        P("fsdp"),
        P("fsdp", None),
        P("fsdp"),
        P("fsdp"),
        P("fsdp"),
        P("fsdp", None),
        P("fsdp"),
        P(None, "fsdp"),
        P("fsdp"),
        P(),
        P(),
        P(),
        P(),
    )
    return jax.shard_map(
        per_device,
        mesh=mesh,
        in_specs=placed,
        out_specs=(
            P("fsdp", None, None),
            P("fsdp", None, None),
            P("fsdp"),
            P("fsdp"),
            P("fsdp", None),
            P("fsdp"),
            P("fsdp", None),
            P("fsdp"),
            P("fsdp"),
            P("fsdp"),
            P("fsdp", None),
            P("fsdp"),
            P(None, "fsdp"),
            P("fsdp"),
            P(),
        ),
        check_vma=False,
    )
```

profile of v0, /device:TPU:0, one launch (start us, length us, event | category | flops | bytes accessed | tf_op | source)
XLA Modules:
  0.0 725.9 jit_solution(5990578621208779468)
XLA Ops:
  18.9 42.4 %all-reduce.17 = (bf16[512]{0:T(512)(128)(2,1)S(1)}, bf16[1024]{0:T(1024)(128)(2,1)S(1)}, bf16[512]{0:T(512)(128)(2,1)S(1)}, bf16[512]{0:T(512)(128)(2,1)S(1)}, ...) all-reduce(bf16[512]{0:T(512)(128)(2,1)S(1)} %dynamic-update-slice., ...), channel_id=1, replica_groups=mesh['fsdp'=32] {'fsdp'}, use_global_device_ids=true, to_apply=%add.3 | all-reduce | flops 6144 | bytes 24576
  66.3 45.4 %all_gather.46 = bf16[512,512]{1,0:T(8,128)(2,1)} all-gather(bf16[16,512]{1,0:T(8,128)(2,1)S(1)} %copy-done.15), channel_id=1, replica_groups=mesh['fsdp'=32] {'fsdp'}, dimensions={0}, use_global_device_ids=true | all-gather | bytes 540672 | tf_op jit(solution)/shard_map/all_gather | solution.py:65
  111.7 2.0 fusion
  116.4 3.0 copy.58
  124.3 1.9 reshape.401
  128.0 3.6 multiply_convert_fusion
  131.6 53.5 %all-gather.8.cloned.1.call-done = bf16[2048,512]{0,1:T(8,128)(2,1)} async-done(((bf16[2048,16]{0,1:T(8,128)(2,1)}), bf16[2048,512]{0,1:T(8,128)(2,1)}) %all-gather.8.cloned.1.call-update) | async-done | bytes 2097168 | tf_op jit(solution)/shard_map/all_gather | solution.py:71
  185.0 3.9 fusion.82
  198.7 2.1 gather.31
  202.0 1.8 multiply_reduce_fusion
  206.9 2.0 pad_maximum_fusion
  208.9 5.8 copy.81
  214.7 4.0 reshape.402
  218.7 2.1 gather_fusion.3
  220.8 3.8 fusion.19
  225.8 2.8 fusion.50
  229.5 2.7 fusion.59
  235.5 2.3 fusion.44
  240.4 39.1 %all-reduce.16 = (f32[512]{0:T(512)S(1)}, f32[512]{0:T(512)S(1)}, f32[1024]{0:T(1024)S(1)}, f32[512]{0:T(512)S(1)}, f32[512]{0:T(512)S(1)}, /*index=5*/f32[512]{...) all-reduce(f32[512]{0:T(512)S(1)} %get-tuple-element.62, ...), channel_id=2, replica_groups=mesh['fsdp'=32] {'fsdp'}, use_global_device_ids=true, to_apply=%region_13.14.clone | all-reduce | flops 8848 | bytes 70784
  284.2 3.2 fusion.16
  287.4 41.9 %reduce-scatter.7.cloned.1.call-done = f32[16,512]{1,0:T(8,128)} async-done(((f32[512,512]{1,0:T(8,128)}), f32[16,512]{1,0:T(8,128)}) %reduce-scatter.7.cloned.1.call-update) | async-done | bytes 32784 | tf_op jit(solution)/shard_map/reduce_scatter | solution.py:99
  329.3 104.0 %reduce-scatter.5.cloned.1.call-done = f32[16,1536]{1,0:T(8,128)} async-done(((f32[512,1536]{1,0:T(8,128)}), f32[16,1536]{1,0:T(8,128)}) %reduce-scatter.5.cloned.1.call-update) | async-done | bytes 98320 | tf_op jit(solution)/shard_map/reduce_scatter | solution.py:97
  433.3 144.1 %reduce-scatter.9.cloned.1.call-done = f32[16,2048]{1,0:T(8,128)} async-done(((f32[512,2048]{1,0:T(8,128)}), f32[16,2048]{1,0:T(8,128)}) %reduce-scatter.9.cloned.1.call-update) | async-done | bytes 131088 | tf_op jit(solution)/shard_map/reduce_scatter | solution.py:103
  577.4 141.6 %reduce-scatter.11.cloned.1.call-done = f32[2048,16]{0,1:T(8,128)} async-done(((f32[2048,512]{0,1:T(8,128)}), f32[2048,16]{0,1:T(8,128)}) %reduce-scatter.11.cloned.1.call-update) | async-done | bytes 131088 | tf_op jit(solution)/shard_map/reduce_scatter | solution.py:105
  (170 shorter events, 52.0 us)
Async XLA Ops:
  7.2 56.0 %copy-start = (bf16[169,16]{0,1:T(8,128)(2,1)S(1)}, bf16[169,16]{0,1:T(8,128)(2,1)}, u32[]{:S(2)}) copy-start(bf16[169,16]{0,1:T(8,128)(2,1)} %param.32) | copy-start | bytes 16228
  7.2 58.7 %copy-start.6 = (bf16[1,196,512]{2,1,0:T(8,128)(2,1)S(1)}, bf16[1,196,512]{2,1,0:T(8,128)(2,1)}, u32[]{:S(2)}) copy-start(bf16[1,196,512]{2,1,0:T(8,128)(2,1)} %param.18) | copy-start | bytes 602116
  7.2 59.1 %copy-start.15 = (bf16[16,512]{1,0:T(8,128)(2,1)S(1)}, bf16[16,512]{1,0:T(8,128)(2,1)}, u32[]{:S(2)}) copy-start(bf16[16,512]{1,0:T(8,128)(2,1)} %param.24) | copy-start | bytes 49156
  7.2 104.5 %all-gather.4.cloned.1.call-start = ((), (), s32[]{:S(2)}) async-start(), calls=%async_computation.4 | async-start | bytes 1622016 | tf_op jit(solution)/shard_map/all_gather | solution.py:63
  7.9 120.0 %all-gather.6.cloned.1.call-start = ((), (), s32[]{:S(2)}) async-start(), calls=%async_computation.5 | async-start | bytes 2162688 | tf_op jit(solution)/shard_map/all_gather | solution.py:69
  8.7 176.3 %all-gather.8.cloned.1.call-start = ((), (), s32[]{:S(2)}) async-start(), calls=%async_computation.6 | async-start | bytes 2162688 | tf_op jit(solution)/shard_map/all_gather | solution.py:71
  9.4 319.9 %reduce-scatter.7.cloned.1.call-start = ((), (), s32[]{:S(2)}) async-start(), calls=%async_computation.8 | async-start | bytes 1081344 | tf_op jit(solution)/shard_map/reduce_scatter | solution.py:99
  63.8 55.6 %copy-start.30 = (pred[4,49]{1,0:T(4,128)(4,1)}, pred[4,49]{1,0:T(4,128)(4,1)S(1)}, u32[]{:S(2)}) copy-start(pred[4,49]{1,0:T(4,128)(4,1)S(1)} %broadcast_in_dim.97) | copy-start | bytes 592
  64.4 49.2 %copy-start.20 = (f32[512]{0:T(512)}, f32[512]{0:T(512)S(1)}, u32[]{:S(2)}) copy-start(f32[512]{0:T(512)S(1)} %convert_element_type.103) | copy-start | bytes 6148
  66.2 61.1 %copy-start.22 = (pred[196]{0:T(512)(128)(4,1)}, pred[196]{0:T(512)(128)(4,1)S(1)}, u32[]{:S(2)}) copy-start(pred[196]{0:T(512)(128)(4,1)S(1)} %compare_and_fusion.1) | copy-start | bytes 592
  66.3 48.5 %copy-start.18 = (f32[196]{0:T(256)}, f32[196]{0:T(256)S(1)}, u32[]{:S(2)}) copy-start(f32[196]{0:T(256)S(1)} %add_rsqrt_fusion.1) | copy-start | bytes 2356
  124.3 3.0 copy-start.7
  124.3 3.0 copy-start.26
  185.0 3.9 copy-start.8
  188.9 3.1 copy-start.23
  193.5 239.8 %reduce-scatter.5.cloned.1.call-start = ((), (), s32[]{:S(2)}) async-start(), calls=%async_computation.7 | async-start | bytes 3244032 | tf_op jit(solution)/shard_map/reduce_scatter | solution.py:97
  195.2 5.5 copy-start.31
  224.6 352.8 %reduce-scatter.9.cloned.1.call-start = ((), (), s32[]{:S(2)}) async-start(), calls=%async_computation.9 | async-start | bytes 4325376 | tf_op jit(solution)/shard_map/reduce_scatter | solution.py:103
  228.6 490.5 %reduce-scatter.11.cloned.1.call-start = ((), (), s32[]{:S(2)}) async-start(), calls=%async_computation.10 | async-start | bytes 4325376 | tf_op jit(solution)/shard_map/reduce_scatter | solution.py:105
  232.2 3.2 copy-start.1
  235.5 2.3 copy-start.5
  238.0 2.3 copy-start.24
  238.1 2.3 copy-start.25
  238.1 2.3 copy-start.27
  (16 other events, 24.6 us)
Sparse Core Ops, SparseCore 0:
  10.9 57.9 all-gather.3
  71.7 55.2 all-gather.5
  130.0 55.0 all-gather.7
  193.6 135.6 reduce-scatter.6
  335.2 98.0 reduce-scatter.4
  436.0 141.3 reduce-scatter.8
  580.3 138.7 reduce-scatter.10
where the time goes:
time: 727 us; the launch traced here: 726 us
  waiting for transfers between devices  487 us (67%)
  blocking collectives  127 us (17%)
  local copies, waits for them, and re-layouts  49.8 us (7%)
  matrix products  35.1 us (5%)
  between operations  14.7 us (2%)
  other arithmetic  11.5 us (2%)
    reduce_scatter x1, waiting for transfers between devices, scatter_whole(): lax.psum_scatter(grads[8], 'fsdp', scatter_dimension=0, tiled=True)  144 us
    reduce_scatter x1, waiting for transfers between devices, scatter_whole(): lax.psum_scatter(grads[10], 'fsdp', scatter_dimension=1, tiled=True)  142 us
    reduce_scatter x1, waiting for transfers between devices, scatter_whole(): lax.psum_scatter(grads[2], 'fsdp', scatter_dimension=0, tiled=True)  104 us
    unnamed x2, blocking collectives  81.6 us
    all_gather x1, waiting for transfers between devices, fetch_pass_fwd(): lax.all_gather(shards[10], 'fsdp', axis=1, tiled=True)  53.5 us
    all_gather x1, blocking collectives, fetch_pass_fwd(): lax.all_gather(shards[4], 'fsdp', axis=0, tiled=True)  45.4 us
    reduce_scatter x1, waiting for transfers between devices, scatter_whole(): lax.psum_scatter(grads[4], 'fsdp', scatter_dimension=0, tiled=True)  41.9 us
    unnamed x91, local copies, waits for them, and re-layouts  16.4 us
  transfers between devices with their start and end apart: 7, of which 5 were waited for; matrix products, arithmetic and copies ran while one was open for 12% of the time, Pallas kernels for 0%

commit v1 on v0

--- a/solution.py
+++ b/solution.py
@@ -11,6 +11,18 @@
 NEG_FILL = -1e30
 ROOT_HALF = 0.7071067811865476
 DENSITY = 0.3989422804014327
+
+
+def doubled_up(value, axis, dim):
+    ways, here = (lax.axis_size(axis), lax.axis_index(axis))
+    grown, reach = (value, 1)
+    while reach < ways:
+        theirs = lax.ppermute(grown, axis, [(d, d ^ reach) for d in range(ways)])
+        mine_first = jnp.concatenate([grown, theirs], axis=dim)
+        theirs_first = jnp.concatenate([theirs, grown], axis=dim)
+        grown = jnp.where(here & reach == 0, mine_first, theirs_first)
+        reach = 2 * reach
+    return grown
 
 
 def normalize(values, gain_vec, shift_vec):
@@ -68,7 +80,7 @@
         lax.all_gather(shards[7], "fsdp", axis=0, tiled=True),
         lax.all_gather(shards[8], "fsdp", axis=0, tiled=True),
         lax.all_gather(shards[9], "fsdp", axis=0, tiled=True),
-        lax.all_gather(shards[10], "fsdp", axis=1, tiled=True),
+        doubled_up(shards[10], "fsdp", 1),
         lax.all_gather(shards[11], "fsdp", axis=0, tiled=True),
     )
 

time: 727 us -> 727 us (level)
  waiting for transfers between devices: 487 us -> 466 us
  blocking collectives: 127 us -> 147 us
    reduce_scatter x1, waiting for transfers between devices: 41.9 us -> 0.01 us  [scatter_whole(): lax.psum_scatter(grads[4], 'fsdp', scatter_dimension=0, tiled=True)]
    ppermute x0 -> x5, waiting for transfers between devices: none -> 23.8 us  [doubled_up(): theirs = lax.ppermute(grown, axis, [(d, d ^ reach) for d in range(ways)])]
    unnamed x2, blocking collectives: 81.6 us -> 105 us
    unnamed x91 -> x71, local copies, waits for them, and re-layouts: 16.4 us -> 15.5 us
  transfers between devices with their start and end apart: 7 -> 12, of which waited for: 5 -> 9; matrix products, arithmetic and copies ran while one was open for 12% -> 11% of each run, Pallas kernels for 0% -> 0%
where the time goes in v1:
time: 727 us
  waiting for transfers between devices  466 us (64%)
  blocking collectives  147 us (20%)
  local copies, waits for them, and re-layouts  46.6 us (6%)
  matrix products  31.5 us (4%)
  between operations  14.6 us (2%)
  other arithmetic  13.8 us (2%)
    reduce_scatter x1, waiting for transfers between devices, scatter_whole(): lax.psum_scatter(grads[8], 'fsdp', scatter_dimension=0, tiled=True)  145 us
    reduce_scatter x1, waiting for transfers between devices, scatter_whole(): lax.psum_scatter(grads[10], 'fsdp', scatter_dimension=1, tiled=True)  141 us
    unnamed x2, blocking collectives  105 us
    reduce_scatter x1, waiting for transfers between devices, scatter_whole(): lax.psum_scatter(grads[2], 'fsdp', scatter_dimension=0, tiled=True)  99.7 us
    all_gather x1, waiting for transfers between devices, fetch_pass_bwd(): lax.all_gather(shards[10], 'fsdp', axis=1, tiled=True)  54.1 us
    all_gather x1, blocking collectives, fetch_pass_fwd(): lax.all_gather(shards[4], 'fsdp', axis=0, tiled=True)  42.1 us
    ppermute x5, waiting for transfers between devices, doubled_up(): theirs = lax.ppermute(grown, axis, [(d, d ^ reach) for d in range(ways)])  23.8 us
    unnamed x71, local copies, waits for them, and re-layouts  15.5 us
  transfers between devices with their start and end apart: 12, of which 9 were waited for; matrix products, arithmetic and copies ran while one was open for 11% of the time, Pallas kernels for 0%

profile of v1, /device:TPU:0, one launch (start us, length us, event | category | flops | bytes accessed | tf_op | source)
XLA Modules:
  0.0 726.5 jit_solution(3827827915900402050)
XLA Ops:
  17.6 42.5 %all-reduce.17 = (bf16[512]{0:T(512)(128)(2,1)S(1)}, bf16[1024]{0:T(1024)(128)(2,1)S(1)}, bf16[512]{0:T(512)(128)(2,1)S(1)}, bf16[512]{0:T(512)(128)(2,1)S(1)}, ...) all-reduce(bf16[512]{0:T(512)(128)(2,1)S(1)} %dynamic-update-slice., ...), channel_id=1, replica_groups=mesh['fsdp'=32] {'fsdp'}, use_global_device_ids=true, to_apply=%add.3 | all-reduce | flops 6144 | bytes 24576
  65.7 42.1 %all_gather.45 = bf16[512,512]{1,0:T(8,128)(2,1)S(1)} all-gather(bf16[16,512]{1,0:T(8,128)(2,1)S(1)} %copy-done.19), channel_id=1, replica_groups=mesh['fsdp'=32] {'fsdp'}, dimensions={0}, use_global_device_ids=true | all-gather | bytes 540672 | tf_op jit(solution)/shard_map/all_gather | solution.py:77
  107.8 2.0 fusion
  109.8 1.9 gather_fusion
  111.7 2.9 reshape.400
  114.7 3.1 copy.58
  127.0 3.9 multiply_convert_fusion
  130.8 54.1 %all-gather.8.cloned.1.call-done = bf16[2048,512]{0,1:T(8,128)(2,1)} async-done(((bf16[2048,16]{0,1:T(8,128)(2,1)}), bf16[2048,512]{0,1:T(8,128)(2,1)}) %all-gather.8.cloned.1.call-update) | async-done | bytes 2097168 | tf_op jit(solution)/shard_map/all_gather | solution.py:100
  184.9 3.8 fusion.91
  196.7 2.1 gather.31
  204.3 4.0 copy.81
  208.2 4.0 reshape.402
  213.3 2.5 fusion.27
  217.1 2.8 fusion.58
  221.1 2.7 fusion.67
  227.4 4.2 collective-permute-done.1
  233.5 6.3 collective-permute-done.2
  242.0 12.3 %collective-permute-done.3 = bf16[2048,128]{0,1:T(8,128)(2,1)} collective-permute-done((bf16[2048,128]{0,1:T(8,128)(2,1)}, bf16[2048,128]{0,1:T(8,128)(2,1)}, u32[]{:S(2)}, u32[]{:S(2)}) %collective-permute-start.3) | collective-permute-done | bytes 524320 | tf_op jit(solution)/shard_map/ppermute | solution.py:20
  254.3 3.0 maximum_select_fusion.10
  262.8 62.7 %all-reduce.16 = (f32[512]{0:T(512)S(1)}, f32[512]{0:T(512)S(1)}, f32[1024]{0:T(1024)S(1)}, f32[512]{0:T(512)S(1)}, f32[512]{0:T(512)S(1)}, /*index=5*/f32[512]{...) all-reduce(f32[512]{0:T(512)} %get-tuple-element.62, ...), channel_id=2, replica_groups=mesh['fsdp'=32] {'fsdp'}, use_global_device_ids=true, to_apply=%region_13.14.clone | all-reduce | flops 8848 | bytes 70784
  330.1 3.8 fusion.24
  334.0 99.7 %reduce-scatter.5.cloned.1.call-done = f32[16,1536]{1,0:T(8,128)} async-done(((f32[512,1536]{1,0:T(8,128)}), f32[16,1536]{1,0:T(8,128)}) %reduce-scatter.5.cloned.1.call-update) | async-done | bytes 98320 | tf_op jit(solution)/shard_map/reduce_scatter | solution.py:109
  433.6 144.6 %reduce-scatter.9.cloned.1.call-done = f32[16,2048]{1,0:T(8,128)} async-done(((f32[512,2048]{1,0:T(8,128)}), f32[16,2048]{1,0:T(8,128)}) %reduce-scatter.9.cloned.1.call-update) | async-done | bytes 131088 | tf_op jit(solution)/shard_map/reduce_scatter | solution.py:115
  578.2 141.5 %reduce-scatter.11.cloned.1.call-done = f32[2048,16]{0,1:T(8,128)} async-done(((f32[2048,512]{0,1:T(8,128)}), f32[2048,16]{0,1:T(8,128)}) %reduce-scatter.11.cloned.1.call-update) | async-done | bytes 131088 | tf_op jit(solution)/shard_map/reduce_scatter | solution.py:117
  (164 shorter events, 59.6 us)
Async XLA Ops:
  7.2 56.0 %copy-start = (bf16[169,16]{0,1:T(8,128)(2,1)S(1)}, bf16[169,16]{0,1:T(8,128)(2,1)}, u32[]{:S(2)}) copy-start(bf16[169,16]{0,1:T(8,128)(2,1)} %param.32) | copy-start | bytes 16228
  7.2 58.1 %copy-start.8 = (bf16[1,196,512]{2,1,0:T(8,128)(2,1)S(1)}, bf16[1,196,512]{2,1,0:T(8,128)(2,1)}, u32[]{:S(2)}) copy-start(bf16[1,196,512]{2,1,0:T(8,128)(2,1)} %param.18) | copy-start | bytes 602116
  7.2 58.5 %copy-start.19 = (bf16[16,512]{1,0:T(8,128)(2,1)S(1)}, bf16[16,512]{1,0:T(8,128)(2,1)}, u32[]{:S(2)}) copy-start(bf16[16,512]{1,0:T(8,128)(2,1)} %param.24) | copy-start | bytes 49156
  7.2 100.6 %all-gather.4.cloned.1.call-start = ((), (), s32[]{:S(2)}) async-start(), calls=%async_computation.4 | async-start | bytes 1622016 | tf_op jit(solution)/shard_map/all_gather | solution.py:75
  7.9 119.0 %all-gather.6.cloned.1.call-start = ((), (), s32[]{:S(2)}) async-start(), calls=%async_computation.5 | async-start | bytes 2162688 | tf_op jit(solution)/shard_map/all_gather | solution.py:81
  8.7 176.2 %all-gather.8.cloned.1.call-start = ((), (), s32[]{:S(2)}) async-start(), calls=%async_computation.6 | async-start | bytes 2162688 | tf_op jit(solution)/shard_map/all_gather | solution.py:100
  9.4 324.5 %reduce-scatter.7.cloned.1.call-start = ((), (), s32[]{:S(2)}) async-start(), calls=%async_computation.8 | async-start | bytes 1081344 | tf_op jit(solution)/shard_map/reduce_scatter | solution.py:111
  61.0 2.8 copy-start.20
  126.0 64.2 %copy-start.1 = (f32[196,512]{1,0:T(8,128)}, f32[196,512]{1,0:T(8,128)S(1)}, u32[]{:S(2)}) copy-start(f32[196,512]{1,0:T(8,128)S(1)} %get-tuple-element.97) | copy-start | bytes 1204228
  126.2 58.7 %copy-start.12 = (bf16[1,196,512]{2,1,0:T(8,128)(2,1)S(1)}, bf16[1,196,512]{2,1,0:T(8,128)(2,1)}, u32[]{:S(2)}) copy-start(bf16[1,196,512]{2,1,0:T(8,128)(2,1)} %param.19) | copy-start | bytes 602116
  184.9 3.8 copy-start.10
  191.0 2.0 copy-start.5
  192.5 241.2 %reduce-scatter.5.cloned.1.call-start = ((), (), s32[]{:S(2)}) async-start(), calls=%async_computation.7 | async-start | bytes 3244032 | tf_op jit(solution)/shard_map/reduce_scatter | solution.py:109
  194.8 5.2 copy-start.4
  215.8 362.4 %reduce-scatter.9.cloned.1.call-start = ((), (), s32[]{:S(2)}) async-start(), calls=%async_computation.9 | async-start | bytes 4325376 | tf_op jit(solution)/shard_map/reduce_scatter | solution.py:115
  219.9 499.8 %reduce-scatter.11.cloned.1.call-start = ((), (), s32[]{:S(2)}) async-start(), calls=%async_computation.10 | async-start | bytes 4325376 | tf_op jit(solution)/shard_map/reduce_scatter | solution.py:117
  224.7 1.3 collective-permute-start
  225.9 5.7 collective-permute-start.1
  231.7 8.1 %collective-permute-start.2 = (bf16[2048,64]{0,1:T(8,128)(2,1)S(1)}, bf16[2048,64]{0,1:T(8,128)(2,1)S(1)}, u32[]{:S(2)}, u32[]{:S(2)}) collective-permute-start(bf16[2048,64]{0,1:T(8,128)(2,1)S(1)} %maximum_select_fusion.12), channel_id=1, source_target_pairs={{0,4},{1,5},{2,6},{3,7},{4,0},{5,1},{6,2},{7,3},{8,12},{9,13},{10,... | collective-permute-start | bytes 786440 | tf_op jit(solution)/shard_map/ppermute | solution.py:20
  240.7 13.5 %collective-permute-start.3 = (bf16[2048,128]{0,1:T(8,128)(2,1)}, bf16[2048,128]{0,1:T(8,128)(2,1)}, u32[]{:S(2)}, u32[]{:S(2)}) collective-permute-start(bf16[2048,128]{0,1:T(8,128)(2,1)} %maximum_select_fusion.11), channel_id=1, source_target_pairs={{0,8},{1,9},{2,10},{3,11},{4,12},{5,13},{6,14},{7,15},{8,0},{9,1},... | collective-permute-start | bytes 1572872 | tf_op jit(solution)/shard_map/ppermute | solution.py:20
  242.0 16.5 %copy-start.22 = (bf16[512,1536]{1,0:T(8,128)(2,1)S(1)}, bf16[512,1536]{1,0:T(8,128)(2,1)}, u32[]{:S(2)}) copy-start(bf16[512,1536]{1,0:T(8,128)(2,1)} %all-gather.4.cloned.1.call-done) | copy-start | bytes 4718596
  257.3 2.6 copy-start.6
  257.3 72.9 %collective-permute-start.4 = (bf16[2048,256]{0,1:T(8,128)(2,1)}, bf16[2048,256]{0,1:T(8,128)(2,1)}, u32[]{:S(2)}, u32[]{:S(2)}) collective-permute-start(bf16[2048,256]{0,1:T(8,128)(2,1)} %maximum_select_fusion.10), channel_id=1, source_target_pairs={{0,16},{1,17},{2,18},{3,19},{4,20},{5,21},{6,22},{7,23},{8,24},{9,... | collective-permute-start | bytes 3145736 | tf_op jit(solution)/shard_map/ppermute | solution.py:20
  260.0 1.8 copy-start.21
  (11 other events, 13.7 us)
Sparse Core Ops, SparseCore 0:
  10.9 57.9 all-gather.3
  71.8 55.1 all-gather.5
  129.8 55.0 all-gather.7
  192.6 136.9 reduce-scatter.6
  335.5 98.1 reduce-scatter.4
  436.4 141.8 reduce-scatter.8
  581.0 138.5 reduce-scatter.10
